TPU v7x, 32 devices: a whole 2x2x4 slice. The times are simulated.
32 devices in a mesh: groups: 2 (over y), blk: 4 (over z), oct: 2 (over x), sub: 2 (over core).
Axes of the slice: x: 2, y: 2, z: 4, core: 2. Of those that a mesh axis runs over, the one named last changes fastest.
Arguments:
- positions: float32 [3, 65536], P(None, ('groups', 'blk', 'oct', 'sub')), parts along dimension 1, may hold values from 0 to 320
- polarizability: float32 [65536], P(('groups', 'blk', 'oct', 'sub')), parts along dimension 0, may hold values from 0.5 to 1.5
- permanent_field: float32 [3, 65536], P(None, ('groups', 'blk', 'oct', 'sub')), parts along dimension 1, may hold values from -40 to 40
- group_id: int32 [65536], P(('groups', 'blk', 'oct', 'sub')), parts along dimension 0, may hold values from 0 to 10921, never falling along the last dimension, each value on 1 to 6 neighbouring positions
- pair_mask: int32 [512, 9], P(('groups', 'blk', 'oct', 'sub')), parts along dimension 0, may hold values from 0 to 1, as said below
Outputs:
- dipoles: float32 [3, 65536], P(None, ('groups', 'blk', 'oct', 'sub')), parts along dimension 1
- residual: float32 [3, 65536], P(None, ('groups', 'blk', 'oct', 'sub')), parts along dimension 1
There are 2 independent parts, one for each index of `groups`. A program takes and returns all parts, laid end to end along the dimension named above; each array names one. Nothing has to cross between parts.
Inputs may be any that keep to these rules, and one draw needn't show every extreme that they name: `group_id`: never falls from one atom to the next; each value names 1 to 6 consecutive atoms. pair_mask[b, 4] = 1, and pair_mask[b, 4 + o] = pair_mask[(b + o) mod 256, 4 - o].
All inputs are finite; a program needn't handle non-finite values.
Results may differ from a plain program's by a relative error of at most 0.0003.
Values sent between devices are 32-bit elements; how exact they have to be, the bound alone decides.
No kernel may reach another device: no remote copies, remote signals or barrier semaphores. Data moves between devices by JAX's collectives and lax.ppermute only.
A program may use at most 64 MiB of HBM per device.

v0:
```python
import math
import jax
import jax.numpy as jnp
import numpy as np
from jax import lax
from jax.sharding import PartitionSpec as P

BOXES_DEV = 2
BLOCK = 128
ORDER = 5
NODE_PAD = 128
ITERS = 2
side_length = 32.0
layer_gap = 2.5
thole_damp = 0.39
highest = lax.Precision.HIGHEST


def padded(cells, sides, width):
    for axis, dim in sides:
        count = lax.axis_size(axis)
        head = lax.slice_in_dim(cells, 0, width, axis=dim)
        tail = lax.slice_in_dim(cells, cells.shape[dim] - width, cells.shape[dim], axis=dim)
        cells = jnp.concatenate(
            [
                lax.ppermute(tail, axis, [(i, (i + 1) % count) for i in range(count)]),
                cells,
                lax.ppermute(head, axis, [((i + 1) % count, i) for i in range(count)]),
            ],
            axis=dim,
        )
    return cells


def wrap_image(delta, period):
    return delta - period * jnp.floor(delta / period + 0.5)


def split_size(total, limit):
    best = 1
    for factor in range(1, min(total, limit) + 1):
        if total % factor == 0:
            best = factor
    return best


def near_tiles(target, source, moments, keep_tile, length_z):
    delta_x = wrap_image(target[0][:, :, None] - source[0][:, None, :], side_length)
    delta_y = wrap_image(target[1][:, :, None] - source[1][:, None, :], side_length)
    delta_z = wrap_image(target[2][:, :, None] - source[2][:, None, :], length_z)
    keep = (keep_tile[:, None, None] > 0.5) & (target[4][:, :, None] != source[4][:, None, :])
    dist_sq = jnp.where(keep, delta_x * delta_x + delta_y * delta_y + delta_z * delta_z, 1.0)
    inv_three = lax.rsqrt(dist_sq) / dist_sq
    scaled = (
        thole_damp
        * dist_sq
        * jnp.sqrt(dist_sq)
        * lax.rsqrt(target[3][:, :, None] * source[3][:, None, :])
    )
    lam_three = -jnp.expm1(-scaled)
    lam_five = lam_three - scaled * jnp.exp(-scaled)
    coef_five = jnp.where(keep, 3.0 * lam_five * inv_three / dist_sq, 0.0)
    coef_three = jnp.where(keep, lam_three * inv_three, 0.0)
    along = (
        delta_x * moments[0][:, None, :]
        + delta_y * moments[1][:, None, :]
        + delta_z * moments[2][:, None, :]
    )
    weighted = coef_five * along
    field_x = jnp.sum(weighted * delta_x - coef_three * moments[0][:, None, :], axis=2)
    field_y = jnp.sum(weighted * delta_y - coef_three * moments[1][:, None, :], axis=2)
    field_z = jnp.sum(weighted * delta_z - coef_three * moments[2][:, None, :], axis=2)
    return jnp.stack([field_x, field_y, field_z])


def near_total(static_ext, dipole_ext, mask_rows, length_z, atom_count):
    reach = (mask_rows.shape[1] - 1) // 2
    width = reach * BLOCK
    blocks = atom_count // BLOCK
    target = static_ext[:, width : width + atom_count].reshape(5, blocks, BLOCK)
    total = jnp.zeros((3, blocks, BLOCK), static_ext.dtype)
    for offset in range(-reach, reach + 1):
        begin = (reach + offset) * BLOCK
        source = static_ext[:, begin : begin + atom_count].reshape(5, blocks, BLOCK)
        moments = dipole_ext[:, begin : begin + atom_count].reshape(3, blocks, BLOCK)
        keep_tile = mask_rows[:, reach + offset].astype(static_ext.dtype)
        total = total + near_tiles(target, source, moments, keep_tile, length_z)
    return total.reshape(3, atom_count)


def node_tables():
    count = ORDER
    roots = np.cos((2.0 * np.arange(count) + 1.0) * np.pi / (2.0 * count))
    degree = np.arange(count)
    coeff = (
        2.0 / count * np.cos(np.outer(2.0 * np.arange(count) + 1.0, degree) * np.pi / (2.0 * count))
    )
    coeff = np.where(degree[None, :] == 0, 1.0 / count, coeff)
    index = np.arange(NODE_PAD)
    live = index < count**3
    safe = np.where(live, index, 0)
    first = safe // (count * count)
    second = safe // count % count
    third = safe % count
    levels = np.arange(count)[None, :]
    pick_a = (first[:, None] == levels) * live[:, None] * 1.0
    pick_b = (second[:, None] == levels) * 1.0
    pick_c = (third[:, None] == levels) * 1.0
    node_x = 16.0 * (1.0 + roots[first])
    node_y = 16.0 * (1.0 + roots[second])
    node_t = roots[third]
    tables = [coeff, pick_a, pick_b, pick_c, node_x, node_y, node_t]
    return [jnp.asarray(item, jnp.float32) for item in tables]


def interpolation(coords, box_ids, box_height):
    coeff, pick_a, pick_b, pick_c, node_x, node_y, node_t = node_tables()
    scaled_x = coords[0] / 16.0 - 1.0
    scaled_y = coords[1] / 16.0 - 1.0
    scaled_z = (
        2.0 * (coords[2] - box_ids.astype(coords.dtype)[:, None] * box_height) / box_height - 1.0
    )

    def basis(values, picks):
        terms = [jnp.ones_like(values), values]
        for degree in range(2, ORDER):
            terms.append(2.0 * values * terms[-1] - terms[-2])
        stacked = jnp.stack(terms[:ORDER])
        smooth = jnp.einsum("kn,nba->kba", coeff, stacked, precision=highest)
        return jnp.einsum("pk,kba->pba", picks, smooth, precision=highest)

    return basis(scaled_x, pick_a) * basis(scaled_y, pick_b) * basis(scaled_z, pick_c)


def far_block(target_ids, source_ids, weights, slabs, box_height, length_z):
    coeff, pick_a, pick_b, pick_c, node_x, node_y, node_t = node_tables()
    height_t = (
        target_ids.astype(weights.dtype)[:, None] * box_height
        + 0.5 * box_height * (1.0 + node_t)[None, :]
    )
    height_s = (
        source_ids.astype(weights.dtype)[:, None] * box_height
        + 0.5 * box_height * (1.0 + node_t)[None, :]
    )
    delta_x = wrap_image(node_x[:, None] - node_x[None, :], side_length)[None, :, None, :]
    delta_y = wrap_image(node_y[:, None] - node_y[None, :], side_length)[None, :, None, :]
    delta_z = wrap_image(height_t[:, :, None, None] - height_s[None, None, :, :], length_z)
    apart = jnp.abs(target_ids[:, None] // BOXES_DEV - source_ids[None, :] // BOXES_DEV)
    apart = jnp.minimum(apart, slabs - apart)
    keep = (apart >= 1)[:, None, :, None]
    dist_sq = jnp.where(
        keep,
        delta_x * delta_x + delta_y * delta_y + delta_z * delta_z + box_height * box_height,
        1.0,
    )
    inv_three = lax.rsqrt(dist_sq) / dist_sq
    coef_five = jnp.where(keep, 3.0 * inv_three / dist_sq, 0.0)
    coef_three = jnp.where(keep, inv_three, 0.0)
    weight_x = weights[:, 0, :][None, None]
    weight_y = weights[:, 1, :][None, None]
    weight_z = weights[:, 2, :][None, None]
    weighted = coef_five * (delta_x * weight_x + delta_y * weight_y + delta_z * weight_z)
    field_x = jnp.sum(weighted * delta_x - coef_three * weight_x, axis=(2, 3))
    field_y = jnp.sum(weighted * delta_y - coef_three * weight_y, axis=(2, 3))
    field_z = jnp.sum(weighted * delta_z - coef_three * weight_z, axis=(2, 3))
    return jnp.stack([field_x, field_y, field_z], axis=1)


def on_device(positions, polarizability, permanent_field, group_id, pair_mask):
    slabs = lax.axis_size(("blk", "oct", "sub"))
    member = lax.axis_index(("blk", "oct", "sub"))
    atom_count = positions.shape[1]
    length_z = layer_gap * atom_count * slabs / 256.0
    box_height = length_z / (BOXES_DEV * slabs)
    per_box = atom_count // BOXES_DEV
    width = (pair_mask.shape[1] - 1) // 2 * BLOCK
    group_limit = max(1, 32 // BOXES_DEV)
    static = jnp.concatenate(
        [positions, polarizability[None, :], group_id.astype(jnp.float32)[None, :]], axis=0
    )
    static_ext = padded(static, ((("blk", "oct", "sub"), 1),), width)
    own_boxes = member * BOXES_DEV + jnp.arange(BOXES_DEV, dtype=jnp.int32)
    interp = interpolation(positions.reshape(3, BOXES_DEV, per_box), own_boxes, box_height)
    surface = 4.0 * math.pi / 3.0 / (side_length * side_length * length_z)

    def induced(dipoles, total):
        dipole_ext = padded(dipoles, ((("blk", "oct", "sub"), 1),), width)
        near = near_total(static_ext, dipole_ext, pair_mask, length_z, atom_count)
        weights = jnp.einsum(
            "pba,cba->bcp", interp, dipoles.reshape(3, BOXES_DEV, per_box), precision=highest
        )
        piece = lax.all_gather(weights, ("blk", "oct", "sub"), axis=0, tiled=True)
        start = jnp.int32(0)
        count = piece.shape[0]
        size = split_size(count, group_limit)
        grouped = piece.reshape(count // size, size, 3, piece.shape[2])

        def visit(acc, item):
            index, bundle = item
            sources = start + index * size + jnp.arange(size, dtype=jnp.int32)
            return (acc + far_block(own_boxes, sources, bundle, slabs, box_height, length_z), None)

        result, unused = lax.scan(
            visit, jnp.zeros_like(weights), (jnp.arange(count // size, dtype=jnp.int32), grouped)
        )
        far = jnp.einsum("pba,bcp->cba", interp, result, precision=highest).reshape(3, atom_count)
        return near + far - surface * total[:, None]

    def moment(values):
        return lax.psum(jnp.sum(values, axis=1), ("blk", "oct", "sub"))

    def squares(resid, scaled):
        return lax.psum(jnp.sum(resid * scaled), ("blk", "oct", "sub"))

    dipoles = polarizability[None, :] * permanent_field
    residual = induced(dipoles, moment(dipoles))
    precond = polarizability[None, :] * residual
    direction = precond
    norm_now = squares(residual, precond)
    for step in range(ITERS):
        image = direction / polarizability[None, :] - induced(direction, moment(direction))
        rate = norm_now / lax.psum(jnp.sum(direction * image), ("blk", "oct", "sub"))
        dipoles = dipoles + rate * direction
        residual = residual - rate * image
        if step + 1 < ITERS:
            precond = polarizability[None, :] * residual
            norm_next = squares(residual, precond)
            direction = precond + norm_next / norm_now * direction
            norm_now = norm_next
    return (dipoles, residual)


def solution(mesh):
    return jax.shard_map(
        on_device,
        mesh=mesh,
        in_specs=(
            P(None, ("groups", "blk", "oct", "sub")),
            P(("groups", "blk", "oct", "sub")),
            P(None, ("groups", "blk", "oct", "sub")),
            P(("groups", "blk", "oct", "sub")),
            P(("groups", "blk", "oct", "sub"), None),
        ),
        out_specs=(
            P(None, ("groups", "blk", "oct", "sub")),
            P(None, ("groups", "blk", "oct", "sub")),
        ),
        check_vma=False,
    )
```

profile of v0, /device:TPU:0, one launch (start us, length us, event | category | flops | bytes accessed | tf_op | source)
XLA Modules:
  0.0 428.3 jit_solution(15247812564218952183)
XLA Ops:
  2.6 5.0 %collective-permute-start.2 = (f32[5,512]{1,0:T(8,128)S(1)}, f32[5,512]{1,0:T(8,128)S(1)}, u32[]{:S(2)}, u32[]{:S(2)}) collective-permute-start(f32[5,512]{1,0:T(8,128)S(1)} %get-tuple-element.990), channel_id=1, source_target_pairs={{1,0},{2,1},{3,2},{4,3},{5,4},{6,5},{7,6},{8,7},{9,8},{10,9},{11,1... | collective-permute-start | bytes 30728 | tf_op jit(solution)/shard_map/ppermute | solution.py:28
  14.0 29.5 %psum.49 = f32[3]{0:T(128)S(1)} all-reduce(f32[3]{0:T(128)S(1)} %get-tuple-element.927), channel_id=1, replica_groups=mesh['groups'=2,'blk'=4,'oct'=2,'sub'=2] {'blk','oct','sub'}, use_global_device_ids=true, to_apply=%region_33.34 | all-reduce | flops 3 | bytes 24 | tf_op jit(solution)/shard_map/psum | solution.py:210
  52.0 17.8 %all_gather.9 = f32[32,3,128]{2,1,0:T(4,128)S(1)} all-gather(f32[2,3,128]{2,1,0:T(4,128)S(1)} %fusion.782), channel_id=1, replica_groups=mesh['groups'=2,'blk'=4,'oct'=2,'sub'=2] {'blk','oct','sub'}, dimensions={0}, use_global_device_ids=true | all-gather | bytes 52224 | tf_op jit(solution)/shard_map/all_gather | solution.py:192
  69.9 13.5 %while.51 = (s32[]{:T(128)}, f32[2,3,128]{2,0,1:T(2,128)S(1)}, s32[2]{0:T(128)S(1)}, f32[2,16,3,128]{3,1,2,0:T(8,128)S(1)}, s32[]{:T(128)}, /*index=5*/s32[]{:T(...) while((s32[]{:T(128)}, f32[2,3,128]{2,0,1:T(2,128)S(1)}, ...), condition=%wide.region_31.32_spmd.clone.clone.clone.clone, body=%wide.region_27.31_spmd.sunk.clone.clone.clone.clone.sunk | while | flops 16765948 | bytes 2795035 | solution.py:203
  71.8 4.8 %subtract_reduce_fusion.9 = (f32[2,128]{1,0:T(2,128)S(1)}, f32[2,128]{1,0:T(2,128)S(1)}, f32[2,128]{1,0:T(2,128)S(1)}) fusion(f32[16,128]{1,0:T(8,128)S(1)} %get-tuple-element.1216, f32[128,128]{1,0:T(8,128)S(1)} %get-tuple-element.1217, pred[2,16]{1,0:T(4,128)(4,1)S(1)} %fusion.814, f32[16,128]{1,0:T(8,128)S(1)} %broadcast_add_fusion.12, ...), kind=kLoop, calls=%fused_computation.28.clone.1 | loop fusion | flops 15727872 | bytes 1282080 | tf_op jit(solution)/shard_map/while/body/eval_jaxpr/reduce_sum | solution.py:163
  78.5 4.8 %subtract_reduce_fusion.9 = (f32[2,128]{1,0:T(2,128)S(1)}, f32[2,128]{1,0:T(2,128)S(1)}, f32[2,128]{1,0:T(2,128)S(1)}) fusion(f32[16,128]{1,0:T(8,128)S(1)} %get-tuple-element.1216, f32[128,128]{1,0:T(8,128)S(1)} %get-tuple-element.1217, pred[2,16]{1,0:T(4,128)(4,1)S(1)} %fusion.814, f32[16,128]{1,0:T(8,128)S(1)} %broadcast_add_fusion.12, ...), kind=kLoop, calls=%fused_computation.28.clone.1 | loop fusion | flops 15727872 | bytes 1282080 | tf_op jit(solution)/shard_map/while/body/eval_jaxpr/reduce_sum | solution.py:163
  112.2 7.3 %fusion.630 = (f32[16,128]{1,0:T(8,128)S(1)}, f32[16,128]{1,0:T(8,128)S(1)}, f32[16,128]{1,0:T(8,128)S(1)}, f32[16,128]{1,0:T(8,128)S(1)}, f32[16,128]{1,0:T(8,128)S(1)}, /*index=5*/f32[16,128]{1,0:T(8,128)S(1)}) fusion(f32[16,128]{1,0:T(8,128)S(1)} %bitcast.840, f32[16,128]{1,0:T(8,128)S(1)} %bitcast.735, f32[16,128]{1,0:T(8,128)S(1)} %bitcast.931, ...), kind=kLoop, calls=%fused_computation.815 | loop fusion | flops 30920704 | bytes 180256 | tf_op jit(solution)/shard_map/reduce_sum | solution.py:70
  120.7 31.6 %psum.51 = f32[3]{0:T(128)S(1)} all-reduce(f32[3]{0:T(128)S(1)} %get-tuple-element.923), channel_id=1, replica_groups=mesh['groups'=2,'blk'=4,'oct'=2,'sub'=2] {'blk','oct','sub'}, use_global_device_ids=true, to_apply=%region_69.70 | all-reduce | flops 3 | bytes 24 | tf_op jit(solution)/shard_map/psum | solution.py:210
  153.2 4.4 %collective-permute-start.5 = (f32[3,512]{1,0:T(4,128)S(1)}, f32[3,512]{1,0:T(4,128)S(1)}, u32[]{:S(2)}, u32[]{:S(2)}) collective-permute-start(f32[3,512]{1,0:T(4,128)S(1)} %get-tuple-element.1078), channel_id=1, source_target_pairs={{1,0},{2,1},{3,2},{4,3},{5,4},{6,5},{7,6},{8,7},{9,8},{10,9},{11,1... | collective-permute-start | bytes 18440 | tf_op jit(solution)/shard_map/ppermute | solution.py:28
  157.6 17.3 %all_gather.10 = f32[32,3,128]{2,1,0:T(4,128)S(1)} all-gather(f32[2,3,128]{2,1,0:T(4,128)S(1)} %fusion.684), channel_id=1, replica_groups=mesh['groups'=2,'blk'=4,'oct'=2,'sub'=2] {'blk','oct','sub'}, dimensions={0}, use_global_device_ids=true | all-gather | bytes 52224 | tf_op jit(solution)/shard_map/all_gather | solution.py:192
  174.9 13.0 %while.52 = (s32[]{:T(128)}, f32[2,3,128]{2,0,1:T(2,128)S(1)}, s32[2]{0:T(128)S(1)}, f32[2,16,3,128]{3,1,2,0:T(8,128)S(1)}, s32[]{:T(128)}, /*index=5*/s32[]{:T(...) while((s32[]{:T(128)}, f32[2,3,128]{2,0,1:T(2,128)S(1)}, ...), condition=%wide.region_67.68_spmd.clone.clone.clone.clone, body=%wide.region_63.67_spmd.sunk.clone.clone.clone.clone.sunk | while | flops 16765948 | bytes 2795035 | solution.py:203
  176.6 4.8 %subtract_reduce_fusion.10 = (f32[2,128]{1,0:T(2,128)S(1)}, f32[2,128]{1,0:T(2,128)S(1)}, f32[2,128]{1,0:T(2,128)S(1)}) fusion(f32[16,128]{1,0:T(8,128)S(1)} %get-tuple-element.1230, f32[128,128]{1,0:T(8,128)S(1)} %get-tuple-element.1231, pred[2,16]{1,0:T(4,128)(4,1)S(1)} %fusion.817, f32[16,128]{1,0:T(8,128)S(1)} %broadcast_add_fusion.14, ...), kind=kLoop, calls=%fused_computation.82.clone.1 | loop fusion | flops 15727872 | bytes 1282080 | tf_op jit(solution)/shard_map/while/body/eval_jaxpr/reduce_sum | solution.py:163
  183.1 4.8 %subtract_reduce_fusion.10 = (f32[2,128]{1,0:T(2,128)S(1)}, f32[2,128]{1,0:T(2,128)S(1)}, f32[2,128]{1,0:T(2,128)S(1)}) fusion(f32[16,128]{1,0:T(8,128)S(1)} %get-tuple-element.1230, f32[128,128]{1,0:T(8,128)S(1)} %get-tuple-element.1231, pred[2,16]{1,0:T(4,128)(4,1)S(1)} %fusion.817, f32[16,128]{1,0:T(8,128)S(1)} %broadcast_add_fusion.14, ...), kind=kLoop, calls=%fused_computation.82.clone.1 | loop fusion | flops 15727872 | bytes 1282080 | tf_op jit(solution)/shard_map/while/body/eval_jaxpr/reduce_sum | solution.py:163
  216.1 7.3 %fusion.629 = (f32[16,128]{1,0:T(8,128)S(1)}, f32[16,128]{1,0:T(8,128)S(1)}, f32[16,128]{1,0:T(8,128)S(1)}, f32[16,128]{1,0:T(8,128)S(1)}, f32[16,128]{1,0:T(8,128)S(1)}, /*index=5*/f32[16,128]{1,0:T(8,128)S(1)}) fusion(f32[16,128]{1,0:T(8,128)S(1)} %bitcast.872, f32[16,128]{1,0:T(8,128)S(1)} %bitcast.736, f32[16,128]{1,0:T(8,128)S(1)} %bitcast.939, ...), kind=kLoop, calls=%fused_computation.814 | loop fusion | flops 30920704 | bytes 180256 | tf_op jit(solution)/shard_map/reduce_sum | solution.py:70
  225.1 32.1 %all-reduce = (f32[]{:T(128)}, f32[]{:T(128)}) all-reduce(f32[]{:T(128)} %get-tuple-element.870, f32[]{:T(128)} %get-tuple-element.869), channel_id=1, replica_groups=mesh['groups'=2,'blk'=4,'oct'=2,'sub'=2] {'blk','oct','sub'}, use_global_device_ids=true, to_apply=%region_35.36 | all-reduce | flops 2 | bytes 16 | tf_op jit(solution)/shard_map/psum | solution.py:213
  259.1 30.1 %psum.53 = f32[]{:T(128)} all-reduce(f32[]{:T(128)} %fusion.632), channel_id=1, replica_groups=mesh['groups'=2,'blk'=4,'oct'=2,'sub'=2] {'blk','oct','sub'}, use_global_device_ids=true, to_apply=%region_73.74 | all-reduce | flops 1 | bytes 8 | tf_op jit(solution)/shard_map/psum | solution.py:213
  290.6 29.7 %psum.54 = f32[3]{0:T(128)S(1)} all-reduce(f32[3]{0:T(128)S(1)} %get-tuple-element.918), channel_id=1, replica_groups=mesh['groups'=2,'blk'=4,'oct'=2,'sub'=2] {'blk','oct','sub'}, use_global_device_ids=true, to_apply=%region_107.108 | all-reduce | flops 3 | bytes 24 | tf_op jit(solution)/shard_map/psum | solution.py:210
  321.3 4.4 %collective-permute-start.7 = (f32[3,512]{1,0:T(4,128)S(1)}, f32[3,512]{1,0:T(4,128)S(1)}, u32[]{:S(2)}, u32[]{:S(2)}) collective-permute-start(f32[3,512]{1,0:T(4,128)S(1)} %get-tuple-element.1070), channel_id=1, source_target_pairs={{1,0},{2,1},{3,2},{4,3},{5,4},{6,5},{7,6},{8,7},{9,8},{10,9},{11,1... | collective-permute-start | bytes 18440 | tf_op jit(solution)/shard_map/ppermute | solution.py:28
  325.7 17.3 %all_gather.11 = f32[32,3,128]{2,1,0:T(4,128)S(1)} all-gather(f32[2,3,128]{2,1,0:T(4,128)S(1)} %fusion.783), channel_id=1, replica_groups=mesh['groups'=2,'blk'=4,'oct'=2,'sub'=2] {'blk','oct','sub'}, dimensions={0}, use_global_device_ids=true | all-gather | bytes 52224 | tf_op jit(solution)/shard_map/all_gather | solution.py:192
  343.0 13.0 %while.53 = (s32[]{:T(128)}, f32[2,3,128]{2,0,1:T(2,128)S(1)}, s32[2]{0:T(128)S(1)}, f32[2,16,3,128]{3,1,2,0:T(8,128)S(1)}, s32[]{:T(128)}, /*index=5*/s32[]{:T(...) while((s32[]{:T(128)}, f32[2,3,128]{2,0,1:T(2,128)S(1)}, ...), condition=%wide.region_105.106_spmd.clone.clone.clone.clone, body=%wide.region_101.105_spmd.sunk.clone.clone.clone.clone.sunk | while | flops 16765948 | bytes 2795035 | solution.py:203
  344.7 4.8 %subtract_reduce_fusion.11 = (f32[2,128]{1,0:T(2,128)S(1)}, f32[2,128]{1,0:T(2,128)S(1)}, f32[2,128]{1,0:T(2,128)S(1)}) fusion(f32[16,128]{1,0:T(8,128)S(1)} %get-tuple-element.1244, f32[128,128]{1,0:T(8,128)S(1)} %get-tuple-element.1245, pred[2,16]{1,0:T(4,128)(4,1)S(1)} %fusion.820, f32[16,128]{1,0:T(8,128)S(1)} %broadcast_add_fusion.16, ...), kind=kLoop, calls=%fused_computation.136.clone.1 | loop fusion | flops 15727872 | bytes 1282080 | tf_op jit(solution)/shard_map/while/body/eval_jaxpr/reduce_sum | solution.py:163
  351.2 4.8 %subtract_reduce_fusion.11 = (f32[2,128]{1,0:T(2,128)S(1)}, f32[2,128]{1,0:T(2,128)S(1)}, f32[2,128]{1,0:T(2,128)S(1)}) fusion(f32[16,128]{1,0:T(8,128)S(1)} %get-tuple-element.1244, f32[128,128]{1,0:T(8,128)S(1)} %get-tuple-element.1245, pred[2,16]{1,0:T(4,128)(4,1)S(1)} %fusion.820, f32[16,128]{1,0:T(8,128)S(1)} %broadcast_add_fusion.16, ...), kind=kLoop, calls=%fused_computation.136.clone.1 | loop fusion | flops 15727872 | bytes 1282080 | tf_op jit(solution)/shard_map/while/body/eval_jaxpr/reduce_sum | solution.py:163
  384.3 7.3 %fusion.628 = (f32[16,128]{1,0:T(8,128)S(1)}, f32[16,128]{1,0:T(8,128)S(1)}, f32[16,128]{1,0:T(8,128)S(1)}, f32[16,128]{1,0:T(8,128)S(1)}, f32[16,128]{1,0:T(8,128)S(1)}, /*index=5*/f32[16,128]{1,0:T(8,128)S(1)}) fusion(f32[16,128]{1,0:T(8,128)S(1)} %bitcast.862, f32[16,128]{1,0:T(8,128)S(1)} %bitcast.737, f32[16,128]{1,0:T(8,128)S(1)} %bitcast.947, ...), kind=kLoop, calls=%fused_computation.813 | loop fusion | flops 30920704 | bytes 180256 | tf_op jit(solution)/shard_map/reduce_sum | solution.py:70
  393.2 32.0 %psum.55 = f32[]{:T(128)} all-reduce(f32[]{:T(128)} %get-tuple-element.1104), channel_id=1, replica_groups=mesh['groups'=2,'blk'=4,'oct'=2,'sub'=2] {'blk','oct','sub'}, use_global_device_ids=true, to_apply=%region_109.110 | all-reduce | flops 1 | bytes 8 | tf_op jit(solution)/shard_map/psum | solution.py:222
  (198 shorter events, 116.9 us)
Async XLA Ops:
  0.6 45.0 %copy-start.8 = (f32[5,5,1]{1,0,2:T(8,128)S(1)}, f32[5,5,1]{1,0,2:T(8,128)}, u32[]{:S(2)}) copy-start(f32[5,5,1]{1,0,2:T(8,128)} %constant.532) | copy-start | bytes 304
  0.6 45.2 %copy-start.11 = (f32[128,5,1]{0,1,2:T(8,128)S(1)}, f32[128,5,1]{0,1,2:T(8,128)}, u32[]{:S(2)}) copy-start(f32[128,5,1]{0,1,2:T(8,128)} %constant.533) | copy-start | bytes 7684
  2.1 81.8 %collective-permute-start = (f32[5,512]{1,0:T(8,128)S(1)}, f32[5,512]{1,0:T(8,128)S(1)}, u32[]{:S(2)}, u32[]{:S(2)}) collective-permute-start(f32[5,512]{1,0:T(8,128)S(1)} %get-tuple-element.989), channel_id=1, source_target_pairs={{0,1},{1,2},{2,3},{3,4},{4,5},{5,6},{6,7},{7,8},{8,9},{9,10},{10,1... | collective-permute-start | bytes 30728 | tf_op jit(solution)/shard_map/ppermute | solution.py:26
  2.6 81.3 %collective-permute-start.2 = (f32[5,512]{1,0:T(8,128)S(1)}, f32[5,512]{1,0:T(8,128)S(1)}, u32[]{:S(2)}, u32[]{:S(2)}) collective-permute-start(f32[5,512]{1,0:T(8,128)S(1)} %get-tuple-element.990), channel_id=1, source_target_pairs={{1,0},{2,1},{3,2},{4,3},{5,4},{6,5},{7,6},{8,7},{9,8},{10,9},{11,1... | collective-permute-start | bytes 30728 | tf_op jit(solution)/shard_map/ppermute | solution.py:28
  8.6 75.2 %collective-permute-start.1 = (f32[3,512]{1,0:T(4,128)S(1)}, f32[3,512]{1,0:T(4,128)S(1)}, u32[]{:S(2)}, u32[]{:S(2)}) collective-permute-start(f32[3,512]{1,0:T(4,128)S(1)} %get-tuple-element.1085), channel_id=1, source_target_pairs={{0,1},{1,2},{2,3},{3,4},{4,5},{5,6},{6,7},{7,8},{8,9},{9,10},{10,1... | collective-permute-start | bytes 18440 | tf_op jit(solution)/shard_map/ppermute | solution.py:26
  8.6 75.2 %collective-permute-start.3 = (f32[3,512]{1,0:T(4,128)S(1)}, f32[3,512]{1,0:T(4,128)S(1)}, u32[]{:S(2)}, u32[]{:S(2)}) collective-permute-start(f32[3,512]{1,0:T(4,128)S(1)} %get-tuple-element.1086), channel_id=1, source_target_pairs={{1,0},{2,1},{3,2},{4,3},{5,4},{6,5},{7,6},{8,7},{9,8},{10,9},{11,1... | collective-permute-start | bytes 18440 | tf_op jit(solution)/shard_map/ppermute | solution.py:28
  13.1 34.7 %copy-start.10 = (f32[128,5,1]{0,1,2:T(8,128)S(1)}, f32[128,5,1]{0,1,2:T(8,128)}, u32[]{:S(2)}) copy-start(f32[128,5,1]{0,1,2:T(8,128)} %constant.534) | copy-start | bytes 7684
  47.7 1.8 copy-start.9
  51.4 18.4 %copy-start.2 = (f32[128]{0:T(128)S(1)}, f32[128]{0:T(128)}, u32[]{:S(2)}) copy-start(f32[128]{0:T(128)} %constant.2011) | copy-start | bytes 1540
  51.4 18.4 %copy-start.4 = (f32[128]{0:T(128)S(1)}, f32[128]{0:T(128)}, u32[]{:S(2)}) copy-start(f32[128]{0:T(128)} %constant.489.clone..sunk.15) | copy-start | bytes 1540
  51.4 18.4 %copy-start.5 = (f32[128]{0:T(128)S(1)}, f32[128]{0:T(128)}, u32[]{:S(2)}) copy-start(f32[128]{0:T(128)} %constant.2010) | copy-start | bytes 1540
  51.4 18.4 %copy-start.6 = (f32[128]{0:T(128)S(1)}, f32[128]{0:T(128)}, u32[]{:S(2)}) copy-start(f32[128]{0:T(128)} %constant.490.clone..sunk.15) | copy-start | bytes 1540
  51.4 18.4 %copy-start.7 = (f32[128]{0:T(128)S(1)}, f32[128]{0:T(128)}, u32[]{:S(2)}) copy-start(f32[128]{0:T(128)} %constant.2009) | copy-start | bytes 1540
  69.9 13.5 %copy-start = (s32[16,9]{1,0:T(8,128)S(1)}, s32[16,9]{1,0:T(8,128)}, u32[]{:S(2)}) copy-start(s32[16,9]{1,0:T(8,128)} %param.28) | copy-start | bytes 1732
  69.9 13.8 %copy-start.1 = (f32[2048]{0:T(1024)S(1)}, f32[2048]{0:T(1024)}, u32[]{:S(2)}) copy-start(f32[2048]{0:T(1024)} %param.25) | copy-start | bytes 24580
  69.9 14.0 %copy-start.3 = (f32[3,2048]{1,0:T(4,128)S(1)}, f32[3,2048]{1,0:T(4,128)}, u32[]{:S(2)}) copy-start(f32[3,2048]{1,0:T(4,128)} %param.24) | copy-start | bytes 73732
  153.1 34.8 %collective-permute-start.4 = (f32[3,512]{1,0:T(4,128)S(1)}, f32[3,512]{1,0:T(4,128)S(1)}, u32[]{:S(2)}, u32[]{:S(2)}) collective-permute-start(f32[3,512]{1,0:T(4,128)S(1)} %get-tuple-element.1077), channel_id=1, source_target_pairs={{0,1},{1,2},{2,3},{3,4},{4,5},{5,6},{6,7},{7,8},{8,9},{9,10},{10,1... | collective-permute-start | bytes 18440 | tf_op jit(solution)/shard_map/ppermute | solution.py:26
  153.2 34.8 %collective-permute-start.5 = (f32[3,512]{1,0:T(4,128)S(1)}, f32[3,512]{1,0:T(4,128)S(1)}, u32[]{:S(2)}, u32[]{:S(2)}) collective-permute-start(f32[3,512]{1,0:T(4,128)S(1)} %get-tuple-element.1078), channel_id=1, source_target_pairs={{1,0},{2,1},{3,2},{4,3},{5,4},{6,5},{7,6},{8,7},{9,8},{10,9},{11,1... | collective-permute-start | bytes 18440 | tf_op jit(solution)/shard_map/ppermute | solution.py:28
  321.2 34.8 %collective-permute-start.6 = (f32[3,512]{1,0:T(4,128)S(1)}, f32[3,512]{1,0:T(4,128)S(1)}, u32[]{:S(2)}, u32[]{:S(2)}) collective-permute-start(f32[3,512]{1,0:T(4,128)S(1)} %get-tuple-element.1069), channel_id=1, source_target_pairs={{0,1},{1,2},{2,3},{3,4},{4,5},{5,6},{6,7},{7,8},{8,9},{9,10},{10,1... | collective-permute-start | bytes 18440 | tf_op jit(solution)/shard_map/ppermute | solution.py:26
  321.3 34.8 %collective-permute-start.7 = (f32[3,512]{1,0:T(4,128)S(1)}, f32[3,512]{1,0:T(4,128)S(1)}, u32[]{:S(2)}, u32[]{:S(2)}) collective-permute-start(f32[3,512]{1,0:T(4,128)S(1)} %get-tuple-element.1070), channel_id=1, source_target_pairs={{1,0},{2,1},{3,2},{4,3},{5,4},{6,5},{7,6},{8,7},{9,8},{10,9},{11,1... | collective-permute-start | bytes 18440 | tf_op jit(solution)/shard_map/ppermute | solution.py:28
where the time goes:
time: 434 us; the launch traced here: 428 us
  blocking collectives  237 us (55%)
  other arithmetic  145 us (33%)
  starting transfers between devices  19 us (4%)
  matrix products  13.6 us (3%)
  between operations  5.61 us (1%)
    reduce_sum x24, other arithmetic, near_tiles(): jnp.sum(weighted * delta_x - coef_three * moments[0][:, None, :], axis=2)  106 us
    psum x3, blocking collectives, moment(): return lax.psum(jnp.sum(values, axis=1), ('blk', 'oct', 'sub'))  90.8 us
    psum x2, blocking collectives, squares(): return lax.psum(jnp.sum(resid * scaled), ('blk', 'oct', 'sub'))  62.2 us
    all_gather x3, blocking collectives, induced(): piece = lax.all_gather(weights, ('blk', 'oct', 'sub'), axis=0, tiled=True)  52.3 us
    psum x1, blocking collectives, on_device(): lax.psum(jnp.sum(direction * image), ('blk', 'oct', 'sub'))  32 us
    reduce_sum x6, other arithmetic, far_block(): field_x = jnp.sum(weighted * delta_x - coef_three * weight_x, axis=(2, 3))  28.8 us
    ppermute x4, starting transfers between devices, padded(): lax.ppermute(head, axis, [((i + 1) % count, i) for i in range(count)])  18.3 us
  transfers between devices with their start and end apart: 8, of which 0 were waited for; matrix products, arithmetic and copies ran while one was open for 11% of the time, Pallas kernels for 0%

commit v1 on v0

--- a/solution.py
+++ b/solution.py
@@ -14,6 +14,23 @@
 layer_gap = 2.5
 thole_damp = 0.39
 highest = lax.Precision.HIGHEST
+
+
+def laid_out(blocks, dim):
+    shape = list(blocks.shape[1:])
+    shape[dim] *= blocks.shape[0]
+    return jnp.moveaxis(blocks, 0, dim).reshape(shape)
+
+
+def ring_gather(x, axis, dim):
+    size = lax.axis_size(axis)
+    right = [(i, (i + 1) % size) for i in range(size)]
+    blocks = [x]
+    while len(blocks) < size:
+        blocks.append(lax.ppermute(blocks[-1], axis, right))
+    index = lax.axis_index(axis)
+    blocks = jnp.stack(blocks)[(index - jnp.arange(size)) % size]
+    return laid_out(blocks, dim)
 
 
 def padded(cells, sides, width):
@@ -189,7 +206,7 @@
         weights = jnp.einsum(
             "pba,cba->bcp", interp, dipoles.reshape(3, BOXES_DEV, per_box), precision=highest
         )
-        piece = lax.all_gather(weights, ("blk", "oct", "sub"), axis=0, tiled=True)
+        piece = ring_gather(weights, ("blk", "oct", "sub"), 0)
         start = jnp.int32(0)
         count = piece.shape[0]
         size = split_size(count, group_limit)

time: 434 us -> 618 us (1.42)
  waiting for transfers between devices: 0.02 us -> 234 us
  blocking collectives: 237 us -> 183 us
    ppermute x0 -> x45, waiting for transfers between devices: none -> 230 us  [ring_gather(): blocks.append(lax.ppermute(blocks[-1], axis, right))]
    all_gather x3 -> x0, blocking collectives: 52.3 us -> none  [induced(): piece = lax.all_gather(weights, ('blk', 'oct', 'sub'), axis=0, tiled=True)]
  transfers between devices with their start and end apart: 8 -> 53, of which waited for: 0 -> 42; matrix products, arithmetic and copies ran while one was open for 11% -> 19% of each run, Pallas kernels for 0% -> 0%
where the time goes in v1:
time: 618 us; the launch traced here: 612 us
  waiting for transfers between devices  234 us (38%)
  blocking collectives  183 us (30%)
  other arithmetic  144 us (23%)
  starting transfers between devices  20.2 us (3%)
  matrix products  13.6 us (2%)
  local copies, waits for them, and re-layouts  6.32 us (1%)
    ppermute x45, waiting for transfers between devices, ring_gather(): blocks.append(lax.ppermute(blocks[-1], axis, right))  230 us
    reduce_sum x24, other arithmetic, near_tiles(): jnp.sum(weighted * delta_x - coef_three * moments[0][:, None, :], axis=2)  106 us
    psum x3, blocking collectives, moment(): return lax.psum(jnp.sum(values, axis=1), ('blk', 'oct', 'sub'))  92.9 us
    psum x2, blocking collectives, squares(): return lax.psum(jnp.sum(resid * scaled), ('blk', 'oct', 'sub'))  60.2 us
    psum x1, blocking collectives, on_device(): lax.psum(jnp.sum(direction * image), ('blk', 'oct', 'sub'))  30.1 us
    reduce_sum x6, other arithmetic, far_block(): field_x = jnp.sum(weighted * delta_x - coef_three * weight_x, axis=(2, 3))  28.8 us
    ppermute x4, starting transfers between devices, padded(): lax.ppermute(head, axis, [((i + 1) % count, i) for i in range(count)])  18.7 us
  transfers between devices with their start and end apart: 53, of which 42 were waited for; matrix products, arithmetic and copies ran while one was open for 19% of the time, Pallas kernels for 0%

profile of v1, /device:TPU:0, one launch (start us, length us, event | category | flops | bytes accessed | tf_op | source)
XLA Modules:
  0.0 611.6 jit_solution(12344325104021943435)
XLA Ops:
  22.6 33.9 %psum.49 = f32[3]{0:T(128)S(1)} all-reduce(f32[3]{0:T(128)S(1)} %get-tuple-element.927), channel_id=1, replica_groups=mesh['groups'=2,'blk'=4,'oct'=2,'sub'=2] {'blk','oct','sub'}, use_global_device_ids=true, to_apply=%region_33.34 | all-reduce | flops 3 | bytes 24 | tf_op jit(solution)/shard_map/psum | solution.py:227
  62.6 5.7 collective-permute-done.6
  92.9 7.3 %fusion.630 = (f32[16,128]{1,0:T(8,128)S(1)}, f32[16,128]{1,0:T(8,128)S(1)}, f32[16,128]{1,0:T(8,128)S(1)}, f32[16,128]{1,0:T(8,128)S(1)}, f32[16,128]{1,0:T(8,128)S(1)}, /*index=5*/f32[16,128]{1,0:T(8,128)S(1)}) fusion(f32[16,128]{1,0:T(8,128)S(1)} %bitcast.941, f32[16,128]{1,0:T(8,128)S(1)} %bitcast.848, f32[16,128]{1,0:T(8,128)S(1)} %bitcast.1028, ...), kind=kLoop, calls=%fused_computation.818 | loop fusion | flops 30920704 | bytes 180256 | tf_op jit(solution)/shard_map/reduce_sum | solution.py:87
  110.0 5.7 collective-permute-done.9
  115.7 5.7 collective-permute-done.10
  121.5 5.7 collective-permute-done.11
  127.2 5.7 collective-permute-done.12
  132.9 5.7 collective-permute-done.13
  138.7 5.7 collective-permute-done.14
  144.4 5.7 collective-permute-done.15
  150.1 5.7 collective-permute-done.16
  155.8 5.7 collective-permute-done.17
  161.6 5.7 collective-permute-done.18
  168.0 13.3 %while.51 = (s32[]{:T(128)}, f32[2,3,128]{2,0,1:T(2,128)S(1)}, s32[2]{0:T(128)S(1)}, f32[2,16,3,128]{3,1,2,0:T(8,128)S(1)}, s32[]{:T(128)}, /*index=5*/s32[]{:T(...) while((s32[]{:T(128)}, f32[2,3,128]{2,0,1:T(2,128)S(1)}, ...), condition=%wide.region_31.32_spmd.clone.clone.clone.clone, body=%wide.region_27.31_spmd.sunk.clone.clone.clone.clone.sunk | while | flops 16765948 | bytes 2795035 | solution.py:220
  182.4 29.5 %psum.51 = f32[3]{0:T(128)S(1)} all-reduce(f32[3]{0:T(128)S(1)} %get-tuple-element.923), channel_id=1, replica_groups=mesh['groups'=2,'blk'=4,'oct'=2,'sub'=2] {'blk','oct','sub'}, use_global_device_ids=true, to_apply=%region_69.70 | all-reduce | flops 3 | bytes 24 | tf_op jit(solution)/shard_map/psum | solution.py:227
  247.1 7.3 %fusion.629 = (f32[16,128]{1,0:T(8,128)S(1)}, f32[16,128]{1,0:T(8,128)S(1)}, f32[16,128]{1,0:T(8,128)S(1)}, f32[16,128]{1,0:T(8,128)S(1)}, f32[16,128]{1,0:T(8,128)S(1)}, /*index=5*/f32[16,128]{1,0:T(8,128)S(1)}) fusion(f32[16,128]{1,0:T(8,128)S(1)} %bitcast.978, f32[16,128]{1,0:T(8,128)S(1)} %bitcast.849, f32[16,128]{1,0:T(8,128)S(1)} %bitcast.1036, ...), kind=kLoop, calls=%fused_computation.817 | loop fusion | flops 30920704 | bytes 180256 | tf_op jit(solution)/shard_map/reduce_sum | solution.py:87
  264.2 5.7 collective-permute-done.24
  333.7 13.3 %while.52 = (s32[]{:T(128)}, f32[2,3,128]{2,0,1:T(2,128)S(1)}, s32[2]{0:T(128)S(1)}, f32[2,16,3,128]{3,1,2,0:T(8,128)S(1)}, s32[]{:T(128)}, /*index=5*/s32[]{:T(...) while((s32[]{:T(128)}, f32[2,3,128]{2,0,1:T(2,128)S(1)}, ...), condition=%wide.region_67.68_spmd.clone.clone.clone.clone, body=%wide.region_63.67_spmd.sunk.clone.clone.clone.clone.sunk | while | flops 16765948 | bytes 2795035 | solution.py:220
  348.6 30.1 %all-reduce = (f32[]{:T(128)}, f32[]{:T(128)}) all-reduce(f32[]{:T(128)} %get-tuple-element.870, f32[]{:T(128)} %get-tuple-element.869), channel_id=1, replica_groups=mesh['groups'=2,'blk'=4,'oct'=2,'sub'=2] {'blk','oct','sub'}, use_global_device_ids=true, to_apply=%region_35.36 | all-reduce | flops 2 | bytes 16 | tf_op jit(solution)/shard_map/psum | solution.py:230
  380.7 30.1 %psum.53 = f32[]{:T(128)} all-reduce(f32[]{:T(128)} %fusion.632), channel_id=1, replica_groups=mesh['groups'=2,'blk'=4,'oct'=2,'sub'=2] {'blk','oct','sub'}, use_global_device_ids=true, to_apply=%region_73.74 | all-reduce | flops 1 | bytes 8 | tf_op jit(solution)/shard_map/psum | solution.py:230
  417.1 29.5 %psum.54 = f32[3]{0:T(128)S(1)} all-reduce(f32[3]{0:T(128)S(1)} %get-tuple-element.918), channel_id=1, replica_groups=mesh['groups'=2,'blk'=4,'oct'=2,'sub'=2] {'blk','oct','sub'}, use_global_device_ids=true, to_apply=%region_107.108 | all-reduce | flops 3 | bytes 24 | tf_op jit(solution)/shard_map/psum | solution.py:227
  477.1 7.3 %fusion.628 = (f32[16,128]{1,0:T(8,128)S(1)}, f32[16,128]{1,0:T(8,128)S(1)}, f32[16,128]{1,0:T(8,128)S(1)}, f32[16,128]{1,0:T(8,128)S(1)}, f32[16,128]{1,0:T(8,128)S(1)}, /*index=5*/f32[16,128]{1,0:T(8,128)S(1)}) fusion(f32[16,128]{1,0:T(8,128)S(1)} %bitcast.969, f32[16,128]{1,0:T(8,128)S(1)} %bitcast.850, f32[16,128]{1,0:T(8,128)S(1)} %bitcast.1044, ...), kind=kLoop, calls=%fused_computation.816 | loop fusion | flops 30920704 | bytes 180256 | tf_op jit(solution)/shard_map/reduce_sum | solution.py:87
  563.8 13.1 %while.53 = (s32[]{:T(128)}, f32[2,3,128]{2,0,1:T(2,128)S(1)}, s32[2]{0:T(128)S(1)}, f32[2,16,3,128]{3,1,2,0:T(8,128)S(1)}, s32[]{:T(128)}, /*index=5*/s32[]{:T(...) while((s32[]{:T(128)}, f32[2,3,128]{2,0,1:T(2,128)S(1)}, ...), condition=%wide.region_105.106_spmd.clone.clone.clone.clone, body=%wide.region_101.105_spmd.sunk.clone.clone.clone.clone.sunk | while | flops 16765948 | bytes 2795035 | solution.py:220
  578.5 30.1 %psum.55 = f32[]{:T(128)} all-reduce(f32[]{:T(128)} %get-tuple-element.1110), channel_id=1, replica_groups=mesh['groups'=2,'blk'=4,'oct'=2,'sub'=2] {'blk','oct','sub'}, use_global_device_ids=true, to_apply=%region_109.110 | all-reduce | flops 1 | bytes 8 | tf_op jit(solution)/shard_map/psum | solution.py:239
  (335 shorter events, 328.0 us)
Async XLA Ops:
  1.6 55.4 %collective-permute-start.3 = (f32[3,512]{1,0:T(4,128)S(1)}, f32[3,512]{1,0:T(4,128)S(1)}, u32[]{:S(2)}, u32[]{:S(2)}) collective-permute-start(f32[3,512]{1,0:T(4,128)S(1)} %get-tuple-element.1086), channel_id=1, source_target_pairs={{1,0},{2,1},{3,2},{4,3},{5,4},{6,5},{7,6},{8,7},{9,8},{10,9},{11,1... | collective-permute-start | bytes 18440 | tf_op jit(solution)/shard_map/ppermute | solution.py:45
  8.5 60.0 %collective-permute-start = (f32[5,512]{1,0:T(8,128)S(1)}, f32[5,512]{1,0:T(8,128)S(1)}, u32[]{:S(2)}, u32[]{:S(2)}) collective-permute-start(f32[5,512]{1,0:T(8,128)S(1)} %get-tuple-element.989), channel_id=1, source_target_pairs={{0,1},{1,2},{2,3},{3,4},{4,5},{5,6},{6,7},{7,8},{8,9},{9,10},{10,1... | collective-permute-start | bytes 30728 | tf_op jit(solution)/shard_map/ppermute | solution.py:43
  8.6 60.0 %collective-permute-start.2 = (f32[5,512]{1,0:T(8,128)S(1)}, f32[5,512]{1,0:T(8,128)S(1)}, u32[]{:S(2)}, u32[]{:S(2)}) collective-permute-start(f32[5,512]{1,0:T(8,128)S(1)} %get-tuple-element.990), channel_id=1, source_target_pairs={{1,0},{2,1},{3,2},{4,3},{5,4},{6,5},{7,6},{8,7},{9,8},{10,9},{11,1... | collective-permute-start | bytes 30728 | tf_op jit(solution)/shard_map/ppermute | solution.py:45
  13.0 43.9 %collective-permute-start.1 = (f32[3,512]{1,0:T(4,128)S(1)}, f32[3,512]{1,0:T(4,128)S(1)}, u32[]{:S(2)}, u32[]{:S(2)}) collective-permute-start(f32[3,512]{1,0:T(4,128)S(1)} %get-tuple-element.1085), channel_id=1, source_target_pairs={{0,1},{1,2},{2,3},{3,4},{4,5},{5,6},{6,7},{7,8},{8,9},{9,10},{10,1... | collective-permute-start | bytes 18440 | tf_op jit(solution)/shard_map/ppermute | solution.py:43
  22.5 34.4 %collective-permute-start.4 = (f32[2,3,128]{2,1,0:T(4,128)S(1)}, f32[2,3,128]{2,1,0:T(4,128)S(1)}, u32[]{:S(2)}, u32[]{:S(2)}) collective-permute-start(f32[2,3,128]{2,1,0:T(4,128)S(1)} %get-tuple-element.1103), channel_id=1, source_target_pairs={{0,1},{1,2},{2,3},{3,4},{4,5},{5,6},{6,7},{7,8},{8,9},{9,10},{10,1... | collective-permute-start | bytes 9224 | tf_op jit(solution)/shard_map/ppermute | solution.py:30
  56.8 5.8 collective-permute-start.5
  62.6 5.7 collective-permute-start.6
  68.4 35.8 %collective-permute-start.7 = (f32[2,3,128]{2,1,0:T(4,128)S(1)}, f32[2,3,128]{2,1,0:T(4,128)S(1)}, u32[]{:S(2)}, u32[]{:S(2)}) collective-permute-start(f32[2,3,128]{2,1,0:T(4,128)S(1)} %collective-permute-done.6), channel_id=1, source_target_pairs={{0,1},{1,2},{2,3},{3,4},{4,5},{5,6},{6,7},{7,8},{8,9},{9,10},{10,1... | collective-permute-start | bytes 9224 | tf_op jit(solution)/shard_map/ppermute | solution.py:30
  104.2 5.8 collective-permute-start.8
  110.0 5.7 collective-permute-start.9
  115.7 5.7 collective-permute-start.10
  121.5 5.7 collective-permute-start.11
  212.7 5.8 collective-permute-start.21
  212.8 6.1 %collective-permute-start.20 = (f32[3,512]{1,0:T(4,128)S(1)}, f32[3,512]{1,0:T(4,128)S(1)}, u32[]{:S(2)}, u32[]{:S(2)}) collective-permute-start(f32[3,512]{1,0:T(4,128)S(1)} %get-tuple-element.1078), channel_id=1, source_target_pairs={{1,0},{2,1},{3,2},{4,3},{5,4},{6,5},{7,6},{8,7},{9,8},{10,9},{11,1... | collective-permute-start | bytes 18440 | tf_op jit(solution)/shard_map/ppermute | solution.py:45
  217.2 5.8 collective-permute-start.19
  218.5 39.9 %collective-permute-start.22 = (f32[2,3,128]{2,1,0:T(4,128)S(1)}, f32[2,3,128]{2,1,0:T(4,128)S(1)}, u32[]{:S(2)}, u32[]{:S(2)}) collective-permute-start(f32[2,3,128]{2,1,0:T(4,128)S(1)} %collective-permute-done.21), channel_id=1, source_target_pairs={{0,1},{1,2},{2,3},{3,4},{4,5},{5,6},{6,7},{7,8},{8,9},{9,10},{10,1... | collective-permute-start | bytes 9224 | tf_op jit(solution)/shard_map/ppermute | solution.py:30
  258.4 5.8 collective-permute-start.23
  327.2 5.9 collective-permute-start.35
  412.6 40.4 %collective-permute-start.36 = (f32[3,512]{1,0:T(4,128)S(1)}, f32[3,512]{1,0:T(4,128)S(1)}, u32[]{:S(2)}, u32[]{:S(2)}) collective-permute-start(f32[3,512]{1,0:T(4,128)S(1)} %get-tuple-element.1069), channel_id=1, source_target_pairs={{0,1},{1,2},{2,3},{3,4},{4,5},{5,6},{6,7},{7,8},{8,9},{9,10},{10,1... | collective-permute-start | bytes 18440 | tf_op jit(solution)/shard_map/ppermute | solution.py:43
  412.6 40.3 %collective-permute-start.37 = (f32[3,512]{1,0:T(4,128)S(1)}, f32[3,512]{1,0:T(4,128)S(1)}, u32[]{:S(2)}, u32[]{:S(2)}) collective-permute-start(f32[3,512]{1,0:T(4,128)S(1)} %get-tuple-element.1070), channel_id=1, source_target_pairs={{1,0},{2,1},{3,2},{4,3},{5,4},{6,5},{7,6},{8,7},{9,8},{10,9},{11,1... | collective-permute-start | bytes 18440 | tf_op jit(solution)/shard_map/ppermute | solution.py:45
  447.1 5.8 collective-permute-start.38
  452.9 35.5 %collective-permute-start.39 = (f32[2,3,128]{2,1,0:T(4,128)S(1)}, f32[2,3,128]{2,1,0:T(4,128)S(1)}, u32[]{:S(2)}, u32[]{:S(2)}) collective-permute-start(f32[2,3,128]{2,1,0:T(4,128)S(1)} %collective-permute-done.38), channel_id=1, source_target_pairs={{0,1},{1,2},{2,3},{3,4},{4,5},{5,6},{6,7},{7,8},{8,9},{9,10},{10,1... | collective-permute-start | bytes 9224 | tf_op jit(solution)/shard_map/ppermute | solution.py:30
  488.4 5.8 collective-permute-start.40
  557.2 5.9 collective-permute-start.52
  (41 other events, 664.0 us)
